TPU v7x, 32 devices: a whole 2x2x4 slice. The times are simulated.
32 devices in a mesh: group: 4 (over x, core), replica: 8 (over z, y).
Axes of the slice: x: 2, y: 2, z: 4, core: 2. Of those that a mesh axis runs over, the one named last changes fastest.
Arguments:
- activations: float32 [16, 1024, 768], P('replica', 'group'), may hold values from -6 to 6
- out_grad: float32 [16, 1024, 768], P('replica', 'group'), may hold values from -6 to 6
- picture_ids: int32 [16, 1024], P('replica'), may hold values from -1 to 9, as said below
- ln1_gain: float32 [768], P('group'), may hold values from 0.5 to 1.5
- ln1_bias: float32 [768], P('group'), may hold values from -3 to 3
- w_query: float32 [768, 768], P(None, 'group'), may hold values from -0.3125 to 0.3125
- q_bias: float32 [768], P('group'), may hold values from -3 to 3
- w_key: float32 [768, 768], P(None, 'group'), may hold values from -0.3125 to 0.3125
- w_value: float32 [768, 768], P(None, 'group'), may hold values from -0.21875 to 0.21875
- v_bias: float32 [768], P('group'), may hold values from -3 to 3
- w_out: float32 [768, 768], P('group'), may hold values from -1.75 to 1.75
- out_bias: float32 [768], P('group'), may hold values from -3 to 3
- ln2_gain: float32 [768], P('group'), may hold values from 0.5 to 1.5
- ln2_bias: float32 [768], P('group'), may hold values from -3 to 3
- w_fc1: float32 [768, 3072], P(None, 'group'), may hold values from -0.21875 to 0.21875
- fc1_bias: float32 [3072], P('group'), may hold values from -3 to 3
- w_fc2: float32 [3072, 768], P('group'), may hold values from -0.109375 to 0.109375
- fc2_bias: float32 [768], P('group'), may hold values from -3 to 3
Outputs:
- output: float32 [16, 1024, 768], P('replica', 'group')
- grad_input: float32 [16, 1024, 768], P('replica', 'group')
- grad_ln1_gain: float32 [768], P('group')
- grad_ln1_bias: float32 [768], P('group')
- grad_w_query: float32 [768, 768], P(None, 'group')
- grad_q_bias: float32 [768], P('group')
- grad_w_key: float32 [768, 768], P(None, 'group')
- grad_w_value: float32 [768, 768], P(None, 'group')
- grad_v_bias: float32 [768], P('group')
- grad_w_out: float32 [768, 768], P('group')
- grad_out_bias: float32 [768], P('group')
- grad_ln2_gain: float32 [768], P('group')
- grad_ln2_bias: float32 [768], P('group')
- grad_w_fc1: float32 [768, 3072], P(None, 'group')
- grad_fc1_bias: float32 [3072], P('group')
- grad_w_fc2: float32 [3072, 768], P('group')
- grad_fc2_bias: float32 [768], P('group')
Inputs may be any that keep to these rules, and one draw needn't show every extreme that they name: `picture_ids`: each row holds whole pictures numbered 0, 1, 2 and so on from its start, each of 100 to 1024 patches, followed by padding marked -1.
All inputs are finite; a program needn't handle non-finite values.
Results may differ from a plain program's by a relative error of at most 0.04.
Values may be sent and summed in bfloat16 or wider, within the bound.
No kernel may reach another device: no remote copies, remote signals or barrier semaphores. Data moves between devices by JAX's collectives and lax.ppermute only.
A program may use at most 256 MiB of HBM per device.

v0:
```python
import jax
import jax.numpy as jnp
from jax import lax
from jax.sharding import PartitionSpec as P

HEADS = 12
HEAD_DIM = 64
EPS = 1e-06
MASKED = -1e30


def to_float(values):
    return values.astype(jnp.float32)


def normalize(values):
    centred = values - jnp.mean(values, axis=-1, keepdims=True)
    inverse = lax.rsqrt(jnp.mean(centred * centred, axis=-1, keepdims=True) + EPS)
    return (centred * inverse, inverse)


def norm_back(grad_hat, normed_hat, inverse):
    return inverse * (
        grad_hat
        - jnp.mean(grad_hat, axis=-1, keepdims=True)
        - normed_hat * jnp.mean(grad_hat * normed_hat, axis=-1, keepdims=True)
    )


def gelu_tanh(values):
    return jax.nn.gelu(values, approximate=True)


def heads_of(values):
    return values.reshape(values.shape[0], HEADS, HEAD_DIM)


def scores_of(query_rows, key_rows, query_ids, key_ids):
    raw_scores = jnp.einsum(
        "qhe,khe->hqk", heads_of(query_rows), heads_of(key_rows), preferred_element_type=jnp.float32
    ) * HEAD_DIM ** (-0.5)
    allowed = query_ids[:, None] == key_ids[None, :]
    return jnp.where(allowed[None], raw_scores, MASKED)


def attend_row(pieces):
    query_rows, key_rows, value_rows, query_ids, key_ids = pieces
    scores = scores_of(query_rows, key_rows, query_ids, key_ids)
    row_top = jnp.max(scores, axis=-1, keepdims=True)
    exponent = jnp.exp(scores - row_top)
    row_total = jnp.sum(exponent, axis=-1, keepdims=True)
    probability = (exponent / row_total).astype(jnp.bfloat16)
    attended = jnp.einsum(
        "hqk,khe->qhe", probability, heads_of(value_rows), preferred_element_type=jnp.float32
    )
    return (
        attended.reshape(query_rows.shape[0], -1).astype(jnp.bfloat16),
        (row_top + jnp.log(row_total))[..., 0],
    )


def attend_back(pieces):
    query_rows, key_rows, value_rows, query_ids, key_ids, logsum, grad_rows = pieces
    scores = scores_of(query_rows, key_rows, query_ids, key_ids)
    probability = jnp.exp(scores - logsum[..., None])
    grad_heads = heads_of(grad_rows)
    grad_value = jnp.einsum(
        "hqk,qhe->khe",
        probability.astype(jnp.bfloat16),
        grad_heads,
        preferred_element_type=jnp.float32,
    )
    grad_probs = jnp.einsum(
        "qhe,khe->hqk", grad_heads, heads_of(value_rows), preferred_element_type=jnp.float32
    )
    centre = jnp.sum(probability * grad_probs, axis=-1, keepdims=True)
    grad_scores = (probability * (grad_probs - centre)).astype(jnp.bfloat16)
    score_scale = HEAD_DIM ** (-0.5)
    grad_query = (
        jnp.einsum(
            "hqk,khe->qhe", grad_scores, heads_of(key_rows), preferred_element_type=jnp.float32
        )
        * score_scale
    )
    grad_key = (
        jnp.einsum(
            "hqk,qhe->khe", grad_scores, heads_of(query_rows), preferred_element_type=jnp.float32
        )
        * score_scale
    )
    query_count = query_rows.shape[0]
    key_count = key_rows.shape[0]
    return (
        grad_query.reshape(query_count, -1).astype(jnp.bfloat16),
        grad_key.reshape(key_count, -1),
        grad_value.reshape(key_count, -1),
    )


def per_device(
    activations,
    out_grad,
    picture_ids,
    ln1_gain,
    ln1_bias,
    w_query,
    q_bias,
    w_key,
    w_value,
    v_bias,
    w_out,
    out_bias,
    ln2_gain,
    ln2_bias,
    w_fc1,
    fc1_bias,
    w_fc2,
    fc2_bias,
):
    row_block, local_len, width = activations.shape
    row_total = row_block * local_len
    offset = lax.axis_index("group") * local_len
    own_ids = lax.dynamic_slice_in_dim(picture_ids, offset, local_len, 1)
    (
        query_full,
        key_full,
        value_full,
        out_full,
        gain_one,
        shift_one,
        bias_query,
        bias_value,
        bias_out,
        gain_two,
        shift_two,
        bias_fc2,
    ) = (
        lax.all_gather(w_query.astype(jnp.bfloat16), "group", axis=1, tiled=True),
        lax.all_gather(w_key.astype(jnp.bfloat16), "group", axis=1, tiled=True),
        lax.all_gather(w_value.astype(jnp.bfloat16), "group", axis=1, tiled=True),
        lax.all_gather(w_out.astype(jnp.bfloat16), "group", axis=0, tiled=True),
        lax.all_gather(ln1_gain.astype(jnp.bfloat16), "group", axis=0, tiled=True),
        lax.all_gather(ln1_bias.astype(jnp.bfloat16), "group", axis=0, tiled=True),
        lax.all_gather(q_bias.astype(jnp.bfloat16), "group", axis=0, tiled=True),
        lax.all_gather(v_bias.astype(jnp.bfloat16), "group", axis=0, tiled=True),
        lax.all_gather(out_bias.astype(jnp.bfloat16), "group", axis=0, tiled=True),
        lax.all_gather(ln2_gain.astype(jnp.bfloat16), "group", axis=0, tiled=True),
        lax.all_gather(ln2_bias.astype(jnp.bfloat16), "group", axis=0, tiled=True),
        lax.all_gather(fc2_bias.astype(jnp.bfloat16), "group", axis=0, tiled=True),
    )
    inputs = activations.reshape(row_total, width)
    hat_one, inverse_one = normalize(inputs)
    normed_one = (hat_one * to_float(gain_one) + to_float(shift_one)).astype(jnp.bfloat16)
    queries = (
        jnp.dot(normed_one, query_full, preferred_element_type=jnp.float32) + to_float(bias_query)
    ).astype(jnp.bfloat16)
    keys_new = jnp.dot(normed_one, key_full, preferred_element_type=jnp.float32).astype(
        jnp.bfloat16
    )
    values_new = (
        jnp.dot(normed_one, value_full, preferred_element_type=jnp.float32) + to_float(bias_value)
    ).astype(jnp.bfloat16)
    key_all, value_all = (
        lax.all_gather(keys_new.reshape(row_block, local_len, width), "group", axis=1, tiled=True),
        lax.all_gather(
            values_new.reshape(row_block, local_len, width), "group", axis=1, tiled=True
        ),
    )
    query_rows = queries.reshape(row_block, local_len, width)
    attended, logsum = lax.map(attend_row, (query_rows, key_all, value_all, own_ids, picture_ids))
    attended = attended.reshape(row_total, width)
    middle = inputs + (
        jnp.dot(attended, out_full, preferred_element_type=jnp.float32) + to_float(bias_out)
    )
    hat_two, inverse_two = normalize(middle)
    normed_two = (hat_two * to_float(gain_two) + to_float(shift_two)).astype(jnp.bfloat16)
    fc1_full, fc2_full, bias_fc1 = (
        lax.all_gather(w_fc1.astype(jnp.bfloat16), "group", axis=1, tiled=True),
        lax.all_gather(w_fc2.astype(jnp.bfloat16), "group", axis=0, tiled=True),
        lax.all_gather(fc1_bias.astype(jnp.bfloat16), "group", axis=0, tiled=True),
    )
    hidden = jnp.dot(normed_two, fc1_full, preferred_element_type=jnp.float32) + to_float(bias_fc1)
    gelu_value, gelu_pull = jax.vjp(gelu_tanh, hidden)
    activated = gelu_value.astype(jnp.bfloat16)
    mlp_output = jnp.dot(activated, fc2_full, preferred_element_type=jnp.float32)
    output = middle + (mlp_output + to_float(bias_fc2))
    valid_rows = (own_ids >= 0).astype(jnp.float32).reshape(row_total, 1)
    grad_out = out_grad.reshape(row_total, width) * valid_rows
    grad_mlp = grad_out.astype(jnp.bfloat16)
    grad_bias_fc2 = jnp.sum(to_float(grad_mlp), axis=0)
    grad_activated = jnp.dot(grad_mlp, fc2_full.T, preferred_element_type=jnp.float32)
    grad_fc2 = jnp.dot(activated.T, grad_mlp, preferred_element_type=jnp.float32)
    grad_hidden = gelu_pull(grad_activated)[0].astype(jnp.bfloat16)
    grad_fc1 = jnp.dot(normed_two.T, grad_hidden, preferred_element_type=jnp.float32)
    grad_bias_fc1 = jnp.sum(to_float(grad_hidden), axis=0)
    grad_normed_two = jnp.dot(grad_hidden, fc1_full.T, preferred_element_type=jnp.float32)
    grad_fc1, grad_fc2, grad_bias_fc1 = (
        lax.psum_scatter(
            grad_fc1.astype(jnp.bfloat16), "group", scatter_dimension=1, tiled=True
        ).astype(jnp.float32),
        lax.psum_scatter(
            grad_fc2.astype(jnp.bfloat16), "group", scatter_dimension=0, tiled=True
        ).astype(jnp.float32),
        lax.psum_scatter(
            grad_bias_fc1.astype(jnp.bfloat16), "group", scatter_dimension=0, tiled=True
        ).astype(jnp.float32),
    )
    grad_gain_two = jnp.sum(grad_normed_two * hat_two, axis=0)
    grad_shift_two = jnp.sum(grad_normed_two, axis=0)
    grad_middle = grad_out + norm_back(grad_normed_two * to_float(gain_two), hat_two, inverse_two)
    grad_branch = grad_middle.astype(jnp.bfloat16)
    grad_bias_out = jnp.sum(to_float(grad_branch), axis=0)
    grad_out_full = jnp.dot(attended.T, grad_branch, preferred_element_type=jnp.float32)
    grad_attended = jnp.dot(grad_branch, out_full.T, preferred_element_type=jnp.float32).astype(
        jnp.bfloat16
    )
    grad_att_rows = grad_attended.reshape(row_block, local_len, width)
    grad_queries, key_parts, value_parts = lax.map(
        attend_back, (query_rows, key_all, value_all, own_ids, picture_ids, logsum, grad_att_rows)
    )
    grad_keys, grad_values = (
        lax.psum_scatter(
            key_parts.astype(jnp.bfloat16), "group", scatter_dimension=1, tiled=True
        ).astype(jnp.float32),
        lax.psum_scatter(
            value_parts.astype(jnp.bfloat16), "group", scatter_dimension=1, tiled=True
        ).astype(jnp.float32),
    )
    grad_queries = grad_queries.reshape(row_total, width)
    grad_keys = grad_keys.reshape(row_total, width).astype(jnp.bfloat16)
    grad_values = grad_values.reshape(row_total, width).astype(jnp.bfloat16)
    grad_query_full = jnp.dot(normed_one.T, grad_queries, preferred_element_type=jnp.float32)
    grad_key_full = jnp.dot(normed_one.T, grad_keys, preferred_element_type=jnp.float32)
    grad_value_full = jnp.dot(normed_one.T, grad_values, preferred_element_type=jnp.float32)
    grad_bias_query = jnp.sum(to_float(grad_queries), axis=0)
    grad_bias_value = jnp.sum(to_float(grad_values), axis=0)
    grad_normed_one = jnp.dot(grad_queries, query_full.T, preferred_element_type=jnp.float32)
    grad_normed_one = grad_normed_one + jnp.dot(
        grad_keys, key_full.T, preferred_element_type=jnp.float32
    )
    grad_normed_one = grad_normed_one + jnp.dot(
        grad_values, value_full.T, preferred_element_type=jnp.float32
    )
    grad_gain_one = jnp.sum(grad_normed_one * hat_one, axis=0)
    grad_shift_one = jnp.sum(grad_normed_one, axis=0)
    grad_input = grad_middle + norm_back(grad_normed_one * to_float(gain_one), hat_one, inverse_one)
    (
        grad_query_full,
        grad_key_full,
        grad_value_full,
        grad_out_full,
        grad_gain_one,
        grad_shift_one,
        grad_bias_query,
        grad_bias_value,
        grad_bias_out,
        grad_gain_two,
        grad_shift_two,
        grad_bias_fc2,
    ) = (
        lax.psum_scatter(
            grad_query_full.astype(jnp.bfloat16), "group", scatter_dimension=1, tiled=True
        ).astype(jnp.float32),
        lax.psum_scatter(
            grad_key_full.astype(jnp.bfloat16), "group", scatter_dimension=1, tiled=True
        ).astype(jnp.float32),
        lax.psum_scatter(
            grad_value_full.astype(jnp.bfloat16), "group", scatter_dimension=1, tiled=True
        ).astype(jnp.float32),
        lax.psum_scatter(
            grad_out_full.astype(jnp.bfloat16), "group", scatter_dimension=0, tiled=True
        ).astype(jnp.float32),
        lax.psum_scatter(
            grad_gain_one.astype(jnp.bfloat16), "group", scatter_dimension=0, tiled=True
        ).astype(jnp.float32),
        lax.psum_scatter(
            grad_shift_one.astype(jnp.bfloat16), "group", scatter_dimension=0, tiled=True
        ).astype(jnp.float32),
        lax.psum_scatter(
            grad_bias_query.astype(jnp.bfloat16), "group", scatter_dimension=0, tiled=True
        ).astype(jnp.float32),
        lax.psum_scatter(
            grad_bias_value.astype(jnp.bfloat16), "group", scatter_dimension=0, tiled=True
        ).astype(jnp.float32),
        lax.psum_scatter(
            grad_bias_out.astype(jnp.bfloat16), "group", scatter_dimension=0, tiled=True
        ).astype(jnp.float32),
        lax.psum_scatter(
            grad_gain_two.astype(jnp.bfloat16), "group", scatter_dimension=0, tiled=True
        ).astype(jnp.float32),
        lax.psum_scatter(
            grad_shift_two.astype(jnp.bfloat16), "group", scatter_dimension=0, tiled=True
        ).astype(jnp.float32),
        lax.psum_scatter(
            grad_bias_fc2.astype(jnp.bfloat16), "group", scatter_dimension=0, tiled=True
        ).astype(jnp.float32),
    )
    (
        grad_query_full,
        grad_key_full,
        grad_value_full,
        grad_out_full,
        grad_gain_one,
        grad_shift_one,
        grad_bias_query,
        grad_bias_value,
        grad_bias_out,
        grad_gain_two,
        grad_shift_two,
        grad_bias_fc2,
        grad_fc1,
        grad_fc2,
        grad_bias_fc1,
    ) = lax.psum(
        (
            grad_query_full,
            grad_key_full,
            grad_value_full,
            grad_out_full,
            grad_gain_one,
            grad_shift_one,
            grad_bias_query,
            grad_bias_value,
            grad_bias_out,
            grad_gain_two,
            grad_shift_two,
            grad_bias_fc2,
            grad_fc1,
            grad_fc2,
            grad_bias_fc1,
        ),
        "replica",
    )
    return (
        output.reshape(row_block, local_len, width),
        grad_input.reshape(row_block, local_len, width),
        grad_gain_one,
        grad_shift_one,
        grad_query_full,
        grad_bias_query,
        grad_key_full,
        grad_value_full,
        grad_bias_value,
        grad_out_full,
        grad_bias_out,
        grad_gain_two,
        grad_shift_two,
        grad_fc1,
        grad_bias_fc1,
        grad_fc2,
        grad_bias_fc2,
    )


def solution(mesh):
    placed = (
        P("replica", "group", None),
        P("replica", "group", None),
        P("replica", None),
        P("group"),
        P("group"),
        P(None, "group"),
        P("group"),
        P(None, "group"),
        P(None, "group"),
        P("group"),
        P("group", None),
        P("group"),
        P("group"),
        P("group"),
        P(None, "group"),
        P("group"),
        P("group", None),
        P("group"),
    )
    return jax.shard_map(
        per_device,
        mesh=mesh,
        in_specs=placed,
        out_specs=(
            P("replica", "group", None),
            P("replica", "group", None),
            P("group"),
            P("group"),
            P(None, "group"),
            P("group"),
            P(None, "group"),
            P(None, "group"),
            P("group"),
            P("group", None),
            P("group"),
            P("group"),
            P("group"),
            P(None, "group"),
            P("group"),
            P("group", None),
            P("group"),
        ),
        check_vma=False,
    )
```

profile of v0, /device:TPU:0, one launch (start us, length us, event | category | flops | bytes accessed | tf_op | source)
XLA Modules:
  0.0 935.0 jit_solution(2342156140588591705)
XLA Ops:
  13.8 13.2 %all-reduce.19 = (bf16[768]{0:T(1024)(128)(2,1)S(1)}, bf16[768]{0:T(1024)(128)(2,1)S(1)}, bf16[768]{0:T(1024)(128)(2,1)S(1)}, bf16[768]{0:T(1024)(128)(2,1)S(1)}...) all-reduce(bf16[768]{0:T(1024)(128)(2,1)S(1)} %dynamic-update-slice, ...), channel_id=1, replica_groups=mesh['group'=4,'replica'=8] {'group'}, use_global_device_ids=true, to_apply=%add.1 | all-reduce | flops 5376 | bytes 21504
  33.9 16.3 %all-gather.16.cloned.1.call-done = bf16[768,768]{0,1:T(8,128)(2,1)} async-done(((bf16[768,192]{0,1:T(8,128)(2,1)}), bf16[768,768]{0,1:T(8,128)(2,1)}) %all-gather.16.cloned.1.call-update) | async-done | bytes 1179664 | tf_op jit(solution)/shard_map/all_gather | solution.py:139
  72.5 28.4 %all-gather.12.cloned.1.call-done = bf16[2,1024,768]{1,2,0:T(8,128)(2,1)} async-done(((bf16[2,256,768]{1,2,0:T(8,128)(2,1)}), bf16[2,1024,768]{1,2,0:T(8,128)(2,1)}) %all-gather.12.cloned.1.call-update) | async-done | bytes 3145744 | tf_op jit(solution)/shard_map/all_gather | solution.py:165
  100.9 30.4 %all-gather.18.cloned.1.call-done = bf16[2,1024,768]{1,2,0:T(8,128)(2,1)} async-done(((bf16[2,256,768]{1,2,0:T(8,128)(2,1)}), bf16[2,1024,768]{1,2,0:T(8,128)(2,1)}) %all-gather.18.cloned.1.call-update) | async-done | bytes 3145744 | tf_op jit(solution)/shard_map/all_gather | solution.py:164
  131.2 29.5 %while.26 = (s32[]{:T(128)}, bf16[2,256,768]{2,1,0:T(8,128)(2,1)}, f32[2,12,256]{2,1,0:T(8,128)}, bf16[2,1024,768]{1,2,0:T(8,128)(2,1)}, s32[2,256]{1,0:T(2,128)...) while((s32[]{:T(128)}, bf16[2,256,768]{2,1,0:T(8,128)(2,1)}, ...), condition=%wide.region_5.6_spmd, body=%wide.region_2.5_spmd.sunk | while | flops 843510784 | bytes 51499116 | solution.py:170
  164.8 25.6 %all-gather.22.cloned.1.call-done = bf16[768,3072]{1,0:T(8,128)(2,1)} async-done(((bf16[768,768]{1,0:T(8,128)(2,1)}), bf16[768,3072]{1,0:T(8,128)(2,1)}) %all-gather.22.cloned.1.call-update) | async-done | bytes 4718608 | tf_op jit(solution)/shard_map/all_gather | solution.py:178
  190.4 8.2 fusion.28
  198.6 31.4 %all-gather.24.cloned.1.call-done = bf16[3072,768]{1,0:T(8,128)(2,1)} async-done(((bf16[768,768]{1,0:T(8,128)(2,1)}), bf16[3072,768]{1,0:T(8,128)(2,1)}) %all-gather.24.cloned.1.call-update) | async-done | bytes 4718608 | tf_op jit(solution)/shard_map/all_gather | solution.py:179
  230.0 9.8 %fusion.29 = (bf16[3072]{0:T(1024)(128)(2,1)}, bf16[512,3072]{1,0:T(8,128)(2,1)S(1)}) fusion(f32[512,3072]{1,0:T(8,128)} %fusion.28, f32[3072]{0:T(1024)S(1)} %bitcast.212, bf16[512,768]{1,0:T(8,128)(2,1)S(1)} %copy-done.22, bf16[3072,768]{1,0:T(8,128)(2,1)} %all-gather.24.cloned.1.call-done), kind=kOutput, calls=%fused_computation.108 | convolution fusion | flops 2450519040 | bytes 14960640 | tf_op jit(solution)/shard_map/dot_general | solution.py:191
  245.7 109.7 %while.27 = (s32[]{:T(128)}, bf16[2,256,768]{1,2,0:T(8,128)(2,1)}, bf16[2,1024,768]{2,1,0:T(8,128)(2,1)}, bf16[2,1024,768]{2,1,0:T(8,128)(2,1)}, bf16[2,1024,768...) while((s32[]{:T(128)}, bf16[2,256,768]{1,2,0:T(8,128)(2,1)}, ...), condition=%wide.region_12.13_spmd, body=%wide.region_10.12_spmd.sunk | while | flops 2062676992 | bytes 238015056 | solution.py:218
  258.3 11.5 %multiply_reduce_fusion.10 = (f32[12,256]{1,0:T(8,128)S(1)}, f32[12,256,1024]{2,1,0:T(8,128)}) fusion(f32[12,256,1024]{2,1,0:T(8,128)} %fusion.113, f32[12,256]{1,0:T(8,128)S(1)} %dynamic-slice_bitcast_fusion.2, pred[256,1024]{1,0:T(8,128)(4,1)S(1)} %broadcast_compare_fusion.5, bf16[256,12,64]{0,2,1:T(8,128)(2,1)S(1)} %bitcast.188, ...), kind=kOutput, calls=%fused_computation.18.clone.1 | convolution fusion | flops 418378752 | bytes 27418624 | tf_op jit(solution)/shard_map/while/body/eval_jaxpr/qhe,khe->hqk/dot_general | solution.py:73
  281.8 9.0 fusion.115
  313.0 11.5 %multiply_reduce_fusion.10 = (f32[12,256]{1,0:T(8,128)S(1)}, f32[12,256,1024]{2,1,0:T(8,128)}) fusion(f32[12,256,1024]{2,1,0:T(8,128)} %fusion.113, f32[12,256]{1,0:T(8,128)S(1)} %dynamic-slice_bitcast_fusion.2, pred[256,1024]{1,0:T(8,128)(4,1)S(1)} %broadcast_compare_fusion.5, bf16[256,12,64]{0,2,1:T(8,128)(2,1)S(1)} %bitcast.188, ...), kind=kOutput, calls=%fused_computation.18.clone.1 | convolution fusion | flops 418378752 | bytes 27418624 | tf_op jit(solution)/shard_map/while/body/eval_jaxpr/qhe,khe->hqk/dot_general | solution.py:73
  336.5 9.0 fusion.115
  364.4 29.1 %reduce-scatter.9.cloned.1.call-done = bf16[2,256,768]{2,1,0:T(8,128)(2,1)} async-done(((bf16[2,1024,768]{2,1,0:T(8,128)(2,1)}), bf16[2,256,768]{2,1,0:T(8,128)(2,1)}) %reduce-scatter.9.cloned.1.call-update) | async-done | bytes 786448 | tf_op jit(solution)/shard_map/reduce_scatter | solution.py:222
  396.9 37.2 %reduce-scatter.11.cloned.1.call-done = bf16[2,256,768]{2,1,0:T(8,128)(2,1)} async-done(((bf16[2,1024,768]{2,1,0:T(8,128)(2,1)}), bf16[2,256,768]{2,1,0:T(8,128)(2,1)}) %reduce-scatter.11.cloned.1.call-update) | async-done | bytes 786448 | tf_op jit(solution)/shard_map/reduce_scatter | solution.py:225
  445.6 8.9 convolution_convert_fusion
  465.4 26.0 %reduce-scatter.19.cloned.1.call-done = bf16[192,768]{1,0:T(8,128)(2,1)} async-done(((bf16[768,768]{1,0:T(8,128)(2,1)}), bf16[192,768]{1,0:T(8,128)(2,1)}) %reduce-scatter.19.cloned.1.call-update) | async-done | bytes 294928 | tf_op jit(solution)/shard_map/reduce_scatter | solution.py:270
  497.7 10.3 %all-reduce.18 = (bf16[768]{0:T(1024)(128)(2,1)S(1)}, bf16[768]{0:T(1024)(128)(2,1)S(1)}, bf16[768]{0:T(1024)(128)(2,1)S(1)}, bf16[768]{0:T(1024)(128)(2,1)S(1)}...) all-reduce(bf16[768]{0:T(1024)(128)(2,1)S(1)} %dynamic-update-slice, ...), channel_id=1, replica_groups=mesh['group'=4,'replica'=8] {'group'}, use_global_device_ids=true, to_apply=%add.7 | all-reduce | flops 9984 | bytes 39936
  511.8 9.3 add_add_fusion.1
  521.1 27.5 %reduce-scatter.17.cloned.1.call-done = bf16[768,192]{0,1:T(8,128)(2,1)} async-done(((bf16[768,768]{0,1:T(8,128)(2,1)}), bf16[768,192]{0,1:T(8,128)(2,1)}) %reduce-scatter.17.cloned.1.call-update) | async-done | bytes 294928 | tf_op jit(solution)/shard_map/reduce_scatter | solution.py:267
  548.6 50.2 %reduce-scatter.21.cloned.1.call-done = bf16[768,768]{1,0:T(8,128)(2,1)} async-done(((bf16[768,3072]{1,0:T(8,128)(2,1)}), bf16[768,768]{1,0:T(8,128)(2,1)}) %reduce-scatter.21.cloned.1.call-update) | async-done | bytes 1179664 | tf_op jit(solution)/shard_map/reduce_scatter | solution.py:198
  598.8 50.5 %reduce-scatter.23.cloned.1.call-done = bf16[768,768]{1,0:T(8,128)(2,1)} async-done(((bf16[3072,768]{1,0:T(8,128)(2,1)}), bf16[768,768]{1,0:T(8,128)(2,1)}) %reduce-scatter.23.cloned.1.call-update) | async-done | bytes 1179664 | tf_op jit(solution)/shard_map/reduce_scatter | solution.py:201
  649.3 279.1 %all-reduce.21 = (f32[192]{0:T(256)}, f32[192]{0:T(256)}, f32[768,192]{0,1:T(8,128)}, f32[192]{0:T(256)}, f32[768,192]{0,1:T(8,128)}, /*index=5*/f32[768,192]{0,...) all-reduce(f32[192]{0:T(256)S(1)} %dynamic-slice_convert_fusion.8, ...), channel_id=1, replica_groups=mesh['group'=4,'replica'=8] {'replica'}, use_global_device_ids=true, to_apply=%region_19.20 | all-reduce | flops 1771776 | bytes 10635264 | tf_op jit(solution)/shard_map/psum | solution.py:314
  (375 shorter events, 184.9 us)
Async XLA Ops:
  7.3 23.3 %all-gather.10.cloned.1.call-start = ((), (), s32[]{:S(2)}) async-start(), calls=%async_computation.8 | async-start | bytes 1474560 | tf_op jit(solution)/shard_map/all_gather | solution.py:140
  9.2 41.0 %all-gather.16.cloned.1.call-start = ((), (), s32[]{:S(2)}) async-start(), calls=%async_computation.11 | async-start | bytes 1474560 | tf_op jit(solution)/shard_map/all_gather | solution.py:139
  10.1 59.8 %all-gather.14.cloned.1.call-start = ((), (), s32[]{:S(2)}) async-start(), calls=%async_computation.10 | async-start | bytes 1474560 | tf_op jit(solution)/shard_map/all_gather | solution.py:138
  10.9 90.0 %all-gather.12.cloned.1.call-start = ((), (), s32[]{:S(2)}) async-start(), calls=%async_computation.9 | async-start | bytes 3932160 | tf_op jit(solution)/shard_map/all_gather | solution.py:165
  33.8 97.4 %all-gather.18.cloned.1.call-start = ((), (), s32[]{:S(2)}) async-start(), calls=%async_computation.12 | async-start | bytes 3932160 | tf_op jit(solution)/shard_map/all_gather | solution.py:164
  53.5 107.2 %all-gather.20.cloned.1.call-start = ((), (), s32[]{:S(2)}) async-start(), calls=%async_computation.13 | async-start | bytes 1474560 | tf_op jit(solution)/shard_map/all_gather | solution.py:141
  54.3 136.0 %all-gather.22.cloned.1.call-start = ((), (), s32[]{:S(2)}) async-start(), calls=%async_computation.14 | async-start | bytes 5898240 | tf_op jit(solution)/shard_map/all_gather | solution.py:178
  57.2 172.7 %all-gather.24.cloned.1.call-start = ((), (), s32[]{:S(2)}) async-start(), calls=%async_computation.15 | async-start | bytes 5898240 | tf_op jit(solution)/shard_map/all_gather | solution.py:179
  60.3 333.3 %reduce-scatter.9.cloned.1.call-start = ((), (), s32[]{:S(2)}) async-start(), calls=%async_computation.16 | async-start | bytes 3932160 | tf_op jit(solution)/shard_map/reduce_scatter | solution.py:222
  61.0 182.3 %copy-start.46 = (f32[768]{0:T(1024)}, f32[768]{0:T(1024)S(1)}, u32[]{:S(2)}) copy-start(f32[768]{0:T(1024)S(1)} %convert_element_type.279) | copy-start | bytes 9220
  61.0 129.4 %copy-start.57 = (f32[768]{0:T(1024)}, f32[768]{0:T(1024)S(1)}, u32[]{:S(2)}) copy-start(f32[768]{0:T(1024)S(1)} %convert_element_type.281) | copy-start | bytes 9220
  163.3 80.0 %copy-start.42 = (f32[512]{0:T(512)}, f32[512]{0:T(512)S(1)}, u32[]{:S(2)}) copy-start(f32[512]{0:T(512)S(1)} %broadcast_multiply_fusion.4) | copy-start | bytes 6148
  164.8 78.5 %copy-start.53 = (f32[512]{0:T(512)}, f32[512]{0:T(512)S(1)}, u32[]{:S(2)}) copy-start(f32[512]{0:T(512)S(1)} %add_rsqrt_fusion) | copy-start | bytes 6148
  164.8 65.2 %copy-start.22 = (bf16[512,768]{1,0:T(8,128)(2,1)S(1)}, bf16[512,768]{1,0:T(8,128)(2,1)}, u32[]{:S(2)}) copy-start(bf16[512,768]{1,0:T(8,128)(2,1)} %fusion.21) | copy-start | bytes 2359300
  164.8 65.2 %copy-start.48 = (f32[4,1,768]{2,1,0:T(1,128)S(1)}, f32[4,1,768]{2,1,0:T(1,128)}, u32[]{:S(2)}) copy-start(f32[4,1,768]{2,1,0:T(1,128)} %convert_element_type.326) | copy-start | bytes 36868
  355.4 78.6 %reduce-scatter.11.cloned.1.call-start = ((), (), s32[]{:S(2)}) async-start(), calls=%async_computation.17 | async-start | bytes 3932160 | tf_op jit(solution)/shard_map/reduce_scatter | solution.py:225
  356.0 109.3 %reduce-scatter.13.cloned.1.call-start = ((), (), s32[]{:S(2)}) async-start(), calls=%async_computation.18 | async-start | bytes 1474560 | tf_op jit(solution)/shard_map/reduce_scatter | solution.py:261
  361.4 130.0 %reduce-scatter.19.cloned.1.call-start = ((), (), s32[]{:S(2)}) async-start(), calls=%async_computation.21 | async-start | bytes 1474560 | tf_op jit(solution)/shard_map/reduce_scatter | solution.py:270
  364.4 156.7 %reduce-scatter.15.cloned.1.call-start = ((), (), s32[]{:S(2)}) async-start(), calls=%async_computation.19 | async-start | bytes 1474560 | tf_op jit(solution)/shard_map/reduce_scatter | solution.py:264
  396.8 151.8 %reduce-scatter.17.cloned.1.call-start = ((), (), s32[]{:S(2)}) async-start(), calls=%async_computation.20 | async-start | bytes 1474560 | tf_op jit(solution)/shard_map/reduce_scatter | solution.py:267
  437.4 161.5 %reduce-scatter.21.cloned.1.call-start = ((), (), s32[]{:S(2)}) async-start(), calls=%async_computation.22 | async-start | bytes 5898240 | tf_op jit(solution)/shard_map/reduce_scatter | solution.py:198
  444.9 204.4 %reduce-scatter.23.cloned.1.call-start = ((), (), s32[]{:S(2)}) async-start(), calls=%async_computation.23 | async-start | bytes 5898240 | tf_op jit(solution)/shard_map/reduce_scatter | solution.py:201
  511.8 137.5 %copy-start.28 = (bf16[768,192]{0,1:T(8,128)(2,1)S(1)}, bf16[768,192]{0,1:T(8,128)(2,1)}, u32[]{:S(2)}) copy-start(bf16[768,192]{0,1:T(8,128)(2,1)} %reduce-scatter.13.cloned.1.call-done) | copy-start | bytes 884740
  511.8 137.5 %copy-start.29 = (bf16[192,768]{1,0:T(8,128)(2,1)S(1)}, bf16[192,768]{1,0:T(8,128)(2,1)}, u32[]{:S(2)}) copy-start(bf16[192,768]{1,0:T(8,128)(2,1)} %reduce-scatter.19.cloned.1.call-done) | copy-start | bytes 884740
  (83 other events, 523.9 us)
Sparse Core Ops, SparseCore 0:
  10.3 20.2 all-gather.9
  32.7 17.4 all-gather.15
  52.3 17.5 all-gather.13
  71.9 28.9 all-gather.11
  102.2 28.9 all-gather.17
  133.2 17.4 all-gather.19
  152.8 37.4 all-gather.21
  192.5 37.4 all-gather.23
  355.6 37.9 reduce-scatter.8
  396.1 37.9 reduce-scatter.10
  437.2 25.7 reduce-scatter.12
  465.6 25.7 reduce-scatter.18
  494.5 25.7 reduce-scatter.14
  522.8 25.7 reduce-scatter.16
  551.0 47.8 reduce-scatter.20
  601.4 47.8 reduce-scatter.22
where the time goes:
time: 942 us; the launch traced here: 935 us
  waiting for transfers between devices  356 us (38%)
  blocking collectives  308 us (33%)
  matrix products  151 us (16%)
  local copies, waits for them, and re-layouts  54.9 us (6%)
  other arithmetic  47.5 us (5%)
  between operations  17 us (2%)
    psum x1, blocking collectives, per_device(): lax.psum((grad_query_full, grad_key_full, grad_value_full, grad_out_full,...  279 us
    reduce_scatter x1, waiting for transfers between devices, per_device(): lax.psum_scatter(grad_fc2.astype(jnp.bfloat16), 'group', scatter_dimensio...  50.5 us
    reduce_scatter x1, waiting for transfers between devices, per_device(): lax.psum_scatter(grad_fc1.astype(jnp.bfloat16), 'group', scatter_dimensio...  50.2 us
    reduce_scatter x1, waiting for transfers between devices, per_device(): lax.psum_scatter(value_parts.astype(jnp.bfloat16), 'group', scatter_dimen...  37.2 us
    all_gather x1, waiting for transfers between devices, per_device(): lax.all_gather(w_fc2.astype(jnp.bfloat16), 'group', axis=0, tiled=True)  31.4 us
    all_gather x1, waiting for transfers between devices, per_device(): lax.all_gather(keys_new.reshape(row_block, local_len, width), 'group', ax...  30.4 us
    reduce_scatter x1, waiting for transfers between devices, per_device(): lax.psum_scatter(key_parts.astype(jnp.bfloat16), 'group', scatter_dimensi...  29.1 us
    all_gather x1, waiting for transfers between devices, per_device(): lax.all_gather(values_new.reshape(row_block, local_len, width), 'group',...  28.4 us
  transfers between devices with their start and end apart: 16, of which 13 were waited for; matrix products, arithmetic and copies ran while one was open for 13% of the time, Pallas kernels for 0%

commit v1 on v0

--- a/solution.py
+++ b/solution.py
@@ -7,6 +7,17 @@
 HEAD_DIM = 64
 EPS = 1e-06
 MASKED = -1e30
+
+
+def gather_around(array, axis, dim):
+    ways = lax.axis_size(axis)
+    pieces = [array]
+    for far in range(1, ways):
+        pieces.append(
+            lax.ppermute(pieces[far - 1], axis, [(d, (d - 1) % ways) for d in range(ways)])
+        )
+    line = jnp.concatenate(pieces, axis=dim)
+    return jnp.roll(line, lax.axis_index(axis) * array.shape[dim], axis=dim)
 
 
 def to_float(values):
@@ -175,7 +186,7 @@
     hat_two, inverse_two = normalize(middle)
     normed_two = (hat_two * to_float(gain_two) + to_float(shift_two)).astype(jnp.bfloat16)
     fc1_full, fc2_full, bias_fc1 = (
-        lax.all_gather(w_fc1.astype(jnp.bfloat16), "group", axis=1, tiled=True),
+        gather_around(w_fc1.astype(jnp.bfloat16), "group", 1),
         lax.all_gather(w_fc2.astype(jnp.bfloat16), "group", axis=0, tiled=True),
         lax.all_gather(fc1_bias.astype(jnp.bfloat16), "group", axis=0, tiled=True),
     )

time: 942 us -> 932 us (0.989)
  waiting for transfers between devices: 356 us -> 291 us
  blocking collectives: 308 us -> 327 us
  local copies, waits for them, and re-layouts: 54.9 us -> 71.5 us
    ppermute x0 -> x3, waiting for transfers between devices: none -> 46.8 us  [gather_around(): lax.ppermute(pieces[far - 1], axis, [(d, (d - 1) % ways) for d in range(w...]
    all_gather x1, waiting for transfers between devices: 30.4 us -> 0.01 us  [per_device(): lax.all_gather(keys_new.reshape(row_block, local_len, width), 'group', ax...]
    all_gather x1, waiting for transfers between devices: 28.4 us -> 0.01 us  [per_device(): lax.all_gather(values_new.reshape(row_block, local_len, width), 'group',...]
    all_gather x1, waiting for transfers between devices: 31.4 us -> 5.8 us  [per_device(): lax.all_gather(w_fc2.astype(jnp.bfloat16), 'group', axis=0, tiled=True)]
    all_gather x1 -> x0, waiting for transfers between devices: 25.6 us -> none  [per_device(): lax.all_gather(w_fc1.astype(jnp.bfloat16), 'group', axis=1, tiled=True)]
    all_gather x1, blocking collectives: 5.2 us -> 24.1 us  [per_device(): lax.all_gather(fc1_bias.astype(jnp.bfloat16), 'group', axis=0, tiled=True)]
    unnamed x143 -> x149, local copies, waits for them, and re-layouts: 7.43 us -> 22.6 us
  transfers between devices with their start and end apart: 16 -> 18, of which waited for: 13 -> 11; matrix products, arithmetic and copies ran while one was open for 13% -> 15% of each run, Pallas kernels for 0% -> 0%
where the time goes in v1:
time: 932 us; the launch traced here: 924 us
  blocking collectives  327 us (35%)
  waiting for transfers between devices  291 us (31%)
  matrix products  154 us (17%)
  local copies, waits for them, and re-layouts  71.5 us (8%)
  other arithmetic  49.1 us (5%)
  between operations  17.2 us (2%)
  loops' own time  9.64 us (1%)
    psum x1, blocking collectives, per_device(): lax.psum((grad_query_full, grad_key_full, grad_value_full, grad_out_full,...  279 us
    reduce_scatter x1, waiting for transfers between devices, per_device(): lax.psum_scatter(grad_fc1.astype(jnp.bfloat16), 'group', scatter_dimensio...  50.4 us
    reduce_scatter x1, waiting for transfers between devices, per_device(): lax.psum_scatter(grad_fc2.astype(jnp.bfloat16), 'group', scatter_dimensio...  50.3 us
    ppermute x3, waiting for transfers between devices, gather_around(): lax.ppermute(pieces[far - 1], axis, [(d, (d - 1) % ways) for d in range(w...  46.8 us
    reduce_scatter x1, waiting for transfers between devices, per_device(): lax.psum_scatter(value_parts.astype(jnp.bfloat16), 'group', scatter_dimen...  37.4 us
    reduce_scatter x1, waiting for transfers between devices, per_device(): lax.psum_scatter(key_parts.astype(jnp.bfloat16), 'group', scatter_dimensi...  29.4 us
    reduce_scatter x1, waiting for transfers between devices, per_device(): lax.psum_scatter(grad_value_full.astype(jnp.bfloat16), 'group', scatter_d...  27.5 us
    reduce_scatter x1, waiting for transfers between devices, per_device(): lax.psum_scatter(grad_out_full.astype(jnp.bfloat16), 'group', scatter_dim...  25.8 us
  transfers between devices with their start and end apart: 18, of which 11 were waited for; matrix products, arithmetic and copies ran while one was open for 15% of the time, Pallas kernels for 0%

profile of v1, /device:TPU:0, one launch (start us, length us, event | category | flops | bytes accessed | tf_op | source)
XLA Modules:
  0.0 923.9 jit_solution(4187839475920406418)
XLA Ops:
  15.0 13.2 %all-reduce.19 = (bf16[768]{0:T(1024)(128)(2,1)S(1)}, bf16[768]{0:T(1024)(128)(2,1)S(1)}, bf16[768]{0:T(1024)(128)(2,1)S(1)}, bf16[768]{0:T(1024)(128)(2,1)S(1)}...) all-reduce(bf16[768]{0:T(1024)(128)(2,1)S(1)} %dynamic-update-slice, ...), channel_id=1, replica_groups=mesh['group'=4,'replica'=8] {'group'}, use_global_device_ids=true, to_apply=%add.1 | all-reduce | flops 5376 | bytes 21504
  33.9 16.3 %all-gather.15.cloned.1.call-done = bf16[768,768]{0,1:T(8,128)(2,1)} async-done(((bf16[768,192]{0,1:T(8,128)(2,1)}), bf16[768,768]{0,1:T(8,128)(2,1)}) %all-gather.15.cloned.1.call-update) | async-done | bytes 1179664 | tf_op jit(solution)/shard_map/all_gather | solution.py:150
  57.9 19.5 %collective-permute-done = bf16[768,768]{1,0:T(8,128)(2,1)} collective-permute-done((bf16[768,768]{1,0:T(8,128)(2,1)}, bf16[768,768]{1,0:T(8,128)(2,1)}, u32[]{:S(2)}, u32[]{:S(2)}) %collective-permute-start) | collective-permute-done | bytes 1179680 | tf_op jit(solution)/shard_map/ppermute | solution.py:17
  83.0 27.3 %collective-permute-done.1 = bf16[768,768]{1,0:T(8,128)(2,1)} collective-permute-done((bf16[768,768]{1,0:T(8,128)(2,1)}, bf16[768,768]{1,0:T(8,128)(2,1)}, u32[]{:S(2)}, u32[]{:S(2)}) %collective-permute-start.1) | collective-permute-done | bytes 1179680 | tf_op jit(solution)/shard_map/ppermute | solution.py:17
  113.5 24.1 %all-gather = bf16[4,1,768]{2,1,0:T(2,128)(2,1)S(1)} all-gather(bf16[1,1,768]{2,1,0:T(2,128)(2,1)S(1)} %reshape.383), channel_id=1, replica_groups=mesh['group'=4,'replica'=8] {'group'}, dimensions={0}, use_global_device_ids=true | all-gather | bytes 7680 | tf_op jit(solution)/shard_map/all_gather | solution.py:191
  159.0 29.9 %while.26 = (s32[]{:T(128)}, bf16[2,256,768]{2,1,0:T(8,128)(2,1)}, f32[2,12,256]{2,1,0:T(8,128)}, bf16[2,1024,768]{1,2,0:T(8,128)(2,1)}, s32[2,256]{1,0:T(2,128)...) while((s32[]{:T(128)}, bf16[2,256,768]{2,1,0:T(8,128)(2,1)}, ...), condition=%wide.region_5.6_spmd, body=%wide.region_2.5_spmd.sunk | while | flops 843510784 | bytes 51499116 | solution.py:181
  192.4 8.0 fusion.22
  206.3 9.7 %fusion.34 = (bf16[3072]{0:T(1024)(128)(2,1)}, bf16[512,3072]{1,0:T(8,128)(2,1)S(1)}) fusion(f32[512,3072]{1,0:T(8,128)} %fusion.22, f32[3072]{0:T(1024)S(1)} %bitcast.210, bf16[512,768]{1,0:T(8,128)(2,1)S(1)} %copy-done.22, bf16[3072,768]{1,0:T(8,128)(2,1)} %all-gather.21.cloned.1.call-done), kind=kOutput, calls=%fused_computation.121 | convolution fusion | flops 2450519040 | bytes 14960640 | tf_op jit(solution)/shard_map/dot_general | solution.py:202
  216.0 7.7 multiply_reduce_fusion.1
  226.9 116.8 %while.27 = (s32[]{:T(128)}, bf16[2,256,768]{1,2,0:T(8,128)(2,1)}, bf16[2,1024,768]{2,1,0:T(8,128)(2,1)}, bf16[2,1024,768]{2,1,0:T(8,128)(2,1)}, bf16[2,1024,768...) while((s32[]{:T(128)}, bf16[2,256,768]{1,2,0:T(8,128)(2,1)}, ...), condition=%wide.region_12.13_spmd, body=%wide.region_10.12_spmd.sunk | while | flops 2062676992 | bytes 238113392 | solution.py:229
  247.2 11.5 %multiply_reduce_fusion.10 = (f32[12,256]{1,0:T(8,128)S(1)}, f32[12,256,1024]{2,1,0:T(8,128)}) fusion(f32[12,256,1024]{2,1,0:T(8,128)} %fusion.116, f32[12,256]{1,0:T(8,128)S(1)} %dynamic-slice_bitcast_fusion.2, pred[256,1024]{1,0:T(8,128)(4,1)S(1)} %broadcast_compare_fusion.5, bf16[256,12,64]{0,2,1:T(8,128)(2,1)S(1)} %bitcast.186, ...), kind=kOutput, calls=%fused_computation.18.clone.1 | convolution fusion | flops 418378752 | bytes 27418624 | tf_op jit(solution)/shard_map/while/body/eval_jaxpr/qhe,khe->hqk/dot_general | solution.py:84
  270.7 9.0 fusion.118
  301.2 11.5 %multiply_reduce_fusion.10 = (f32[12,256]{1,0:T(8,128)S(1)}, f32[12,256,1024]{2,1,0:T(8,128)}) fusion(f32[12,256,1024]{2,1,0:T(8,128)} %fusion.116, f32[12,256]{1,0:T(8,128)S(1)} %dynamic-slice_bitcast_fusion.2, pred[256,1024]{1,0:T(8,128)(4,1)S(1)} %broadcast_compare_fusion.5, bf16[256,12,64]{0,2,1:T(8,128)(2,1)S(1)} %bitcast.186, ...), kind=kOutput, calls=%fused_computation.18.clone.1 | convolution fusion | flops 418378752 | bytes 27418624 | tf_op jit(solution)/shard_map/while/body/eval_jaxpr/qhe,khe->hqk/dot_general | solution.py:84
  324.6 9.0 fusion.118
  352.5 29.4 %reduce-scatter.9.cloned.1.call-done = bf16[2,256,768]{2,1,0:T(8,128)(2,1)} async-done(((bf16[2,1024,768]{2,1,0:T(8,128)(2,1)}), bf16[2,256,768]{2,1,0:T(8,128)(2,1)}) %reduce-scatter.9.cloned.1.call-update) | async-done | bytes 786448 | tf_op jit(solution)/shard_map/reduce_scatter | solution.py:233
  385.3 37.4 %reduce-scatter.11.cloned.1.call-done = bf16[2,256,768]{2,1,0:T(8,128)(2,1)} async-done(((bf16[2,1024,768]{2,1,0:T(8,128)(2,1)}), bf16[2,256,768]{2,1,0:T(8,128)(2,1)}) %reduce-scatter.11.cloned.1.call-update) | async-done | bytes 786448 | tf_op jit(solution)/shard_map/reduce_scatter | solution.py:236
  425.9 8.8 convolution_convert_fusion
  454.1 25.8 %reduce-scatter.19.cloned.1.call-done = bf16[192,768]{1,0:T(8,128)(2,1)} async-done(((bf16[768,768]{1,0:T(8,128)(2,1)}), bf16[192,768]{1,0:T(8,128)(2,1)}) %reduce-scatter.19.cloned.1.call-update) | async-done | bytes 294928 | tf_op jit(solution)/shard_map/reduce_scatter | solution.py:281
  486.2 10.3 %all-reduce.18 = (bf16[768]{0:T(1024)(128)(2,1)S(1)}, bf16[768]{0:T(1024)(128)(2,1)S(1)}, bf16[768]{0:T(1024)(128)(2,1)S(1)}, bf16[768]{0:T(1024)(128)(2,1)S(1)}...) all-reduce(bf16[768]{0:T(1024)(128)(2,1)S(1)} %dynamic-update-slice, ...), channel_id=1, replica_groups=mesh['group'=4,'replica'=8] {'group'}, use_global_device_ids=true, to_apply=%add.7 | all-reduce | flops 9984 | bytes 39936
  500.4 9.3 %add_add_fusion.1 = f32[512,768]{1,0:T(8,128)} fusion(f32[512,768]{1,0:T(8,128)S(1)} %copy-done.16, bf16[3072,768]{1,0:T(8,128)(2,1)} %all-gather.21.cloned.1.call-done, f32[768]{0:T(1024)S(1)} %convert_element_type.289, f32[512,3072]{1,0:T(8,128)} %fusion.22, f32[3072]{0:T(1024)S(1)} %bitcast.212), kind=kOutput, calls=%fused_computation.71 | convolution fusion | flops 2432434176 | bytes 14171136 | tf_op jit(solution)/shard_map/dot_general | solution.py:196
  509.7 27.5 %reduce-scatter.17.cloned.1.call-done = bf16[768,192]{0,1:T(8,128)(2,1)} async-done(((bf16[768,768]{0,1:T(8,128)(2,1)}), bf16[768,192]{0,1:T(8,128)(2,1)}) %reduce-scatter.17.cloned.1.call-update) | async-done | bytes 294928 | tf_op jit(solution)/shard_map/reduce_scatter | solution.py:278
  537.2 50.3 %reduce-scatter.23.cloned.1.call-done = bf16[768,768]{1,0:T(8,128)(2,1)} async-done(((bf16[3072,768]{1,0:T(8,128)(2,1)}), bf16[768,768]{1,0:T(8,128)(2,1)}) %reduce-scatter.23.cloned.1.call-update) | async-done | bytes 1179664 | tf_op jit(solution)/shard_map/reduce_scatter | solution.py:212
  587.4 50.4 %reduce-scatter.21.cloned.1.call-done = bf16[768,768]{1,0:T(8,128)(2,1)} async-done(((bf16[768,3072]{1,0:T(8,128)(2,1)}), bf16[768,768]{1,0:T(8,128)(2,1)}) %reduce-scatter.21.cloned.1.call-update) | async-done | bytes 1179664 | tf_op jit(solution)/shard_map/reduce_scatter | solution.py:209
  637.9 279.1 %all-reduce.21 = (f32[192]{0:T(256)}, f32[192]{0:T(256)}, f32[768,192]{0,1:T(8,128)}, f32[192]{0:T(256)}, f32[768,192]{0,1:T(8,128)}, /*index=5*/f32[768,192]{0,...) all-reduce(f32[192]{0:T(256)S(1)} %dynamic-slice_convert_fusion.8, ...), channel_id=1, replica_groups=mesh['group'=4,'replica'=8] {'replica'}, use_global_device_ids=true, to_apply=%region_19.20 | all-reduce | flops 1771776 | bytes 10635264 | tf_op jit(solution)/shard_map/psum | solution.py:325
  (389 shorter events, 201.8 us)
Async XLA Ops:
  7.3 23.3 %all-gather.9.cloned.1.call-start = ((), (), s32[]{:S(2)}) async-start(), calls=%async_computation.8 | async-start | bytes 1474560 | tf_op jit(solution)/shard_map/all_gather | solution.py:151
  9.3 40.9 %all-gather.15.cloned.1.call-start = ((), (), s32[]{:S(2)}) async-start(), calls=%async_computation.11 | async-start | bytes 1474560 | tf_op jit(solution)/shard_map/all_gather | solution.py:150
  11.2 130.4 %all-gather.13.cloned.1.call-start = ((), (), s32[]{:S(2)}) async-start(), calls=%async_computation.10 | async-start | bytes 1474560 | tf_op jit(solution)/shard_map/all_gather | solution.py:149
  12.0 146.9 %all-gather.11.cloned.1.call-start = ((), (), s32[]{:S(2)}) async-start(), calls=%async_computation.9 | async-start | bytes 3932160 | tf_op jit(solution)/shard_map/all_gather | solution.py:176
  33.9 125.1 %all-gather.17.cloned.1.call-start = ((), (), s32[]{:S(2)}) async-start(), calls=%async_computation.12 | async-start | bytes 3932160 | tf_op jit(solution)/shard_map/all_gather | solution.py:175
  53.6 135.3 %all-gather.19.cloned.1.call-start = ((), (), s32[]{:S(2)}) async-start(), calls=%async_computation.13 | async-start | bytes 1474560 | tf_op jit(solution)/shard_map/all_gather | solution.py:152
  56.9 20.5 %collective-permute-start = (bf16[768,768]{1,0:T(8,128)(2,1)}, bf16[768,768]{1,0:T(8,128)(2,1)}, u32[]{:S(2)}, u32[]{:S(2)}) collective-permute-start(bf16[768,768]{1,0:T(8,128)(2,1)} %get-tuple-element.266), channel_id=1, source_target_pairs={{0,24},{8,0},{16,8},{24,16},{1,25},{9,1},{17,9},{25,17},{2,26},{10... | collective-permute-start | bytes 3538952 | tf_op jit(solution)/shard_map/ppermute | solution.py:17
  57.9 55.5 %copy-start.57 = (f32[768]{0:T(1024)S(1)}, f32[768]{0:T(1024)}, u32[]{:S(2)}) copy-start(f32[768]{0:T(1024)} %param.37) | copy-start | bytes 9220
  57.9 80.3 %copy-start.12 = (f32[2,256,768]{2,1,0:T(8,128)S(1)}, f32[2,256,768]{2,1,0:T(8,128)}, u32[]{:S(2)}) copy-start(f32[2,256,768]{2,1,0:T(8,128)} %param.23) | copy-start | bytes 4718596
  57.9 148.4 %all-gather.21.cloned.1.call-start = ((), (), s32[]{:S(2)}) async-start(), calls=%async_computation.14 | async-start | bytes 5898240 | tf_op jit(solution)/shard_map/all_gather | solution.py:190
  77.5 32.8 %collective-permute-start.1 = (bf16[768,768]{1,0:T(8,128)(2,1)}, bf16[768,768]{1,0:T(8,128)(2,1)}, u32[]{:S(2)}, u32[]{:S(2)}) collective-permute-start(bf16[768,768]{1,0:T(8,128)(2,1)} %collective-permute-done), channel_id=1, source_target_pairs={{0,24},{8,0},{16,8},{24,16},{1,25},{9,1},{17,9},{25,17},{2,26},{10... | collective-permute-start | bytes 3538952 | tf_op jit(solution)/shard_map/ppermute | solution.py:17
  82.2 299.7 %reduce-scatter.9.cloned.1.call-start = ((), (), s32[]{:S(2)}) async-start(), calls=%async_computation.15 | async-start | bytes 3932160 | tf_op jit(solution)/shard_map/reduce_scatter | solution.py:233
  82.9 140.7 %copy-start.47 = (f32[768]{0:T(1024)}, f32[768]{0:T(1024)S(1)}, u32[]{:S(2)}) copy-start(f32[768]{0:T(1024)S(1)} %convert_element_type.279) | copy-start | bytes 9220
  82.9 108.7 %copy-start.58 = (f32[768]{0:T(1024)}, f32[768]{0:T(1024)S(1)}, u32[]{:S(2)}) copy-start(f32[768]{0:T(1024)S(1)} %convert_element_type.281) | copy-start | bytes 9220
  110.3 36.2 %collective-permute-start.2 = (bf16[768,768]{1,0:T(8,128)(2,1)}, bf16[768,768]{1,0:T(8,128)(2,1)}, u32[]{:S(2)}, u32[]{:S(2)}) collective-permute-start(bf16[768,768]{1,0:T(8,128)(2,1)} %collective-permute-done.1), channel_id=1, source_target_pairs={{0,24},{8,0},{16,8},{24,16},{1,25},{9,1},{17,9},{25,17},{2,26},{10... | collective-permute-start | bytes 3538952 | tf_op jit(solution)/shard_map/ppermute | solution.py:17
  343.9 78.8 %reduce-scatter.11.cloned.1.call-start = ((), (), s32[]{:S(2)}) async-start(), calls=%async_computation.16 | async-start | bytes 3932160 | tf_op jit(solution)/shard_map/reduce_scatter | solution.py:236
  344.6 109.5 %reduce-scatter.13.cloned.1.call-start = ((), (), s32[]{:S(2)}) async-start(), calls=%async_computation.17 | async-start | bytes 1474560 | tf_op jit(solution)/shard_map/reduce_scatter | solution.py:272
  349.4 130.5 %reduce-scatter.19.cloned.1.call-start = ((), (), s32[]{:S(2)}) async-start(), calls=%async_computation.20 | async-start | bytes 1474560 | tf_op jit(solution)/shard_map/reduce_scatter | solution.py:281
  352.5 157.2 %reduce-scatter.15.cloned.1.call-start = ((), (), s32[]{:S(2)}) async-start(), calls=%async_computation.18 | async-start | bytes 1474560 | tf_op jit(solution)/shard_map/reduce_scatter | solution.py:275
  385.2 152.0 %reduce-scatter.17.cloned.1.call-start = ((), (), s32[]{:S(2)}) async-start(), calls=%async_computation.19 | async-start | bytes 1474560 | tf_op jit(solution)/shard_map/reduce_scatter | solution.py:278
  425.9 161.5 %reduce-scatter.23.cloned.1.call-start = ((), (), s32[]{:S(2)}) async-start(), calls=%async_computation.22 | async-start | bytes 5898240 | tf_op jit(solution)/shard_map/reduce_scatter | solution.py:212
  434.8 203.0 %reduce-scatter.21.cloned.1.call-start = ((), (), s32[]{:S(2)}) async-start(), calls=%async_computation.21 | async-start | bytes 5898240 | tf_op jit(solution)/shard_map/reduce_scatter | solution.py:209
  500.4 137.5 %copy-start.28 = (bf16[768,192]{0,1:T(8,128)(2,1)S(1)}, bf16[768,192]{0,1:T(8,128)(2,1)}, u32[]{:S(2)}) copy-start(bf16[768,192]{0,1:T(8,128)(2,1)} %reduce-scatter.13.cloned.1.call-done) | copy-start | bytes 884740
  500.4 137.5 %copy-start.29 = (bf16[192,768]{1,0:T(8,128)(2,1)S(1)}, bf16[192,768]{1,0:T(8,128)(2,1)}, u32[]{:S(2)}) copy-start(bf16[192,768]{1,0:T(8,128)(2,1)} %reduce-scatter.19.cloned.1.call-done) | copy-start | bytes 884740
  (87 other events, 627.7 us)
Sparse Core Ops, SparseCore 0:
  10.3 20.3 all-gather.8
  32.8 17.4 all-gather.14
  52.4 20.6 all-gather.12
  75.1 37.4 all-gather.10
  114.0 33.1 all-gather.16
  149.1 17.4 all-gather.18
  168.8 37.4 all-gather.20
  343.9 37.9 reduce-scatter.8
  384.7 37.9 reduce-scatter.10
  425.6 25.7 reduce-scatter.12
  454.2 25.7 reduce-scatter.18
  482.9 25.7 reduce-scatter.14
  511.4 25.7 reduce-scatter.16
  539.5 47.8 reduce-scatter.22
  590.0 47.8 reduce-scatter.20
